TPU v7x, 256 devices: a whole 4x4x8 slice. The times are simulated.
256 devices in a mesh: dp: 4 (over x), expert: 64 (over z, y, core).
Axes of the slice: x: 4, y: 4, z: 8, core: 2. Of those that a mesh axis runs over, the one named last changes fastest.
Arguments:
- cell_table: bfloat16 [524288, 256], P(('dp', 'expert')), may hold values from -6 to 6
- sample_index: int32 [262144], P(('dp', 'expert')), may hold values from 0 to 2047
- region: int32 [262144, 1], P(('dp', 'expert')), may hold values from 0 to 63; in each aligned block of 1024 rows (0 to 1023, 1024 to 2047, ...) at most 32 rows name the same one
- targets: bfloat16 [262144, 256], P(('dp', 'expert')), may hold values from -6 to 6
- trunk_weight: bfloat16 [256, 256], replicated, may hold values from -0.375 to 0.375
- expert_params: float32 [64, 2, 256, 2048], P('expert', None, None, 'dp'), may hold values from -0.375 to 0.375
- first_moment: float32 [64, 2, 256, 2048], P('expert', None, None, 'dp'), may hold values from -4 to 4
- second_moment: float32 [64, 2, 256, 2048], P('expert', None, None, 'dp'), may hold values from 0.05 to 1
Outputs:
- trunk_grad: float32 [256, 256], replicated
- row_loss: float32 [262144], P(('dp', 'expert'))
- new_params: float32 [64, 2, 256, 2048], P('expert', None, None, 'dp')
- new_first: float32 [64, 2, 256, 2048], P('expert', None, None, 'dp')
- new_second: float32 [64, 2, 256, 2048], P('expert', None, None, 'dp')
Inputs may be any that keep to these rules, and one draw needn't show every extreme that they name: In the 1024 rows of one device no region is named more than 32 times; some region exactly 32 times. `sample_index`: indexes the rows of the same device's block of cell_table.
All inputs are finite; a program needn't handle non-finite values.
Results may differ from a plain program's by a relative error of at most 0.0044.
Values may be sent and summed in bfloat16 or wider, within the bound.
A program may use at most 128 MiB of HBM per device.

v0:
```python
import jax
import jax.numpy as jnp
from jax import lax
from jax.sharding import PartitionSpec as P

loss_scale = 1.0 / 32.0
beta_one = 0.9
beta_two = 0.999
learn_rate = 0.05
adam_eps = 1e-08
adam_step = 10


def silu_slope(values):
    sigma = jax.nn.sigmoid(values)
    return sigma * (1.0 + values * (1.0 - sigma))


def adam_update(params, first, second, grads):
    first_new = beta_one * first + (1.0 - beta_one) * grads
    second_new = beta_two * second + (1.0 - beta_two) * grads * grads
    first_hat = first_new / (1.0 - beta_one**adam_step)
    second_hat = second_new / (1.0 - beta_two**adam_step)
    return (
        params - learn_rate * first_hat / (jnp.sqrt(second_hat) + adam_eps),
        first_new,
        second_new,
    )


def on_device(
    cell_table,
    sample_index,
    region,
    targets,
    trunk_weight,
    expert_params,
    first_moment,
    second_moment,
):
    rows = sample_index.shape[0]
    width = cell_table.shape[1]
    experts = lax.axis_size("expert")
    capacity = 2 * rows // experts
    features = jnp.take(cell_table, sample_index, axis=0)
    routed = region[:, 0]
    onehot = (routed[:, None] == jnp.arange(experts, dtype=jnp.int32)[None, :]).astype(jnp.int32)
    slots = jnp.sum(jnp.cumsum(onehot, axis=0) * onehot, axis=1) - 1
    places = routed * capacity + slots
    gathered = lax.all_gather(expert_params.astype(jnp.bfloat16), "dp", axis=3, tiled=True)
    w_up = gathered[0, 0]
    w_down = gathered[0, 1]
    payload = jnp.concatenate([features, targets], axis=1)
    packed = jnp.zeros((experts * capacity, 2 * width), jnp.bfloat16).at[places].set(payload)
    arrived = lax.all_to_all(
        packed.reshape(experts, capacity, 2 * width),
        "expert",
        split_axis=0,
        concat_axis=0,
        tiled=True,
    ).reshape(-1, 2 * width)
    feats = arrived[:, :width]
    there = arrived[:, width:]
    trunk_pre = jnp.dot(feats, trunk_weight, preferred_element_type=jnp.float32)
    trunk_out = (feats.astype(jnp.float32) + jax.nn.silu(trunk_pre)).astype(jnp.bfloat16)
    up_pre = jnp.dot(trunk_out, w_up, preferred_element_type=jnp.float32)
    hidden = jax.nn.silu(up_pre).astype(jnp.bfloat16)
    predicted = lax.dot_general(
        hidden, w_down, (((1,), (1,)), ((), ())), preferred_element_type=jnp.float32
    )
    errors = predicted - there.astype(jnp.float32)
    losses = jnp.sum(errors * errors, axis=1) * (0.5 * loss_scale)
    scaled = (errors * loss_scale).astype(jnp.bfloat16)
    back = lax.all_to_all(
        losses.reshape(experts, capacity), "expert", split_axis=0, concat_axis=0, tiled=True
    )
    row_loss = back.reshape(-1)[places]
    grad_down = lax.dot_general(
        scaled, hidden, (((0,), (0,)), ((), ())), preferred_element_type=jnp.float32
    )
    hidden_grad = jnp.dot(scaled, w_down, preferred_element_type=jnp.float32)
    pre_grad = (hidden_grad * silu_slope(up_pre)).astype(jnp.bfloat16)
    grad_up = lax.dot_general(
        trunk_out, pre_grad, (((0,), (0,)), ((), ())), preferred_element_type=jnp.float32
    )
    row_grad = lax.dot_general(
        pre_grad, w_up, (((1,), (1,)), ((), ())), preferred_element_type=jnp.float32
    ).astype(jnp.bfloat16)
    trunk_slope = (row_grad.astype(jnp.float32) * silu_slope(trunk_pre)).astype(jnp.bfloat16)
    trunk_local = lax.dot_general(
        feats, trunk_slope, (((0,), (0,)), ((), ())), preferred_element_type=jnp.float32
    )
    trunk_grad = lax.psum(trunk_local, ("dp", "expert"))
    grads = jnp.stack([grad_up, grad_down])[None]
    grad_shard = lax.psum_scatter(grads, "dp", scatter_dimension=3, tiled=True)
    new_params, new_first, new_second = adam_update(
        expert_params, first_moment, second_moment, grad_shard
    )
    return (trunk_grad, row_loss, new_params, new_first, new_second)


def solution(mesh):
    placed = (
        P(("dp", "expert"), None),
        P(("dp", "expert")),
        P(("dp", "expert"), None),
        P(("dp", "expert"), None),
        P(),
        P("expert", None, None, "dp"),
        P("expert", None, None, "dp"),
        P("expert", None, None, "dp"),
    )
    return jax.shard_map(
        on_device,
        mesh=mesh,
        in_specs=placed,
        out_specs=(
            P(),
            P(("dp", "expert")),
            P("expert", None, None, "dp"),
            P("expert", None, None, "dp"),
            P("expert", None, None, "dp"),
        ),
        check_vma=False,
    )
```

profile of v0, /device:TPU:2, one launch (start us, length us, event | category | flops | bytes accessed | tf_op | source)
XLA Modules:
  0.0 451.5 jit_solution(14048339895175946293)
XLA Ops:
  7.2 0.0 copy-start
  7.2 0.0 copy-start.6
  7.2 0.8 fusion.17
  8.0 0.7 compare_and_fusion
  8.7 0.7 fusion.16
  9.4 18.0 %reduce-window.6 = s32[64,8,128]{2,1,0:T(8,128)S(1)} reduce-window(s32[64,8,128]{2,1,0:T(8,128)S(1)} %fusion.16, s32[]{:T(128)} %constant.20.clone.1), window={size=1x1x128 pad=0_0x0_0x127_0}, to_apply=%region_0.1 | reduce-window | flops 8323072 | bytes 524292 | tf_op jit(solution)/shard_map/reduce-window
  27.4 0.1 slice.28
  27.5 0.1 copy.17
  27.7 0.1 copy.18
  27.8 0.1 broadcast_add_fusion
  27.9 0.0 copy-done.6
  27.9 0.1 fusion.15
  28.0 0.0 copy-done
  28.1 0.0 copy-start.4
  28.1 3.9 gather_fusion
  32.0 0.2 broadcast_select_fusion
  32.2 0.0 copy-done.4
  32.2 6.7 %scatter_custom_fusion = bf16[2048,512]{1,0:T(8,128)(2,1)} fusion(s32[1024]{0:T(1024)S(1)} %bitcast.54, bf16[1024,256]{1,0:T(8,128)(2,1)S(1)} %copy-done.4, bf16[]{:T(256)} %constant.67, bf16[1024,256]{1,0:T(8,128)(2,1)S(1)} %broadcast_select_fusion, bf16[]{:T(256)} %constant.18.clone.1), kind=kCustom, calls=%fused_computation.22 | custom fusion | flops 2097152 | bytes 3145732 | tf_op jit(solution)/shard_map/scatter | solution.py:54
  38.9 12.1 %all-to-all-start = ((bf16[64,32,512]{2,1,0:T(8,128)(2,1)}), bf16[64,32,512]{2,1,0:T(8,128)(2,1)S(1)}, u32[]{:S(2)}, u32[]{:S(2)}) async-start(bf16[64,32,512]{2,1,0:T(8,128)(2,1)} %bitcast.6), calls=%async_computation | async-start | bytes 4194304 | tf_op jit(solution)/shard_map/all_to_all | solution.py:55
  51.0 0.0 copy-start.5
  51.1 0.0 all-gather.2.cloned.1.call-start
  51.1 2.1 convert_element_type.38
  53.2 0.0 all-gather.2.cloned.1.call-update
  53.2 0.2 reduce-scatter.2.cloned.1.call-start
  53.5 48.9 %all-to-all-done = bf16[64,32,512]{2,1,0:T(8,128)(2,1)S(1)} async-done(((bf16[64,32,512]{2,1,0:T(8,128)(2,1)}), bf16[64,32,512]{2,1,0:T(8,128)(2,1)S(1)}, u32[]{:S(2)}, u32[]{:S(2)}) %all-to-all-start) | async-done | bytes 2097184 | tf_op jit(solution)/shard_map/all_to_all | solution.py:55
  102.4 0.0 copy-done.5
  102.4 1.7 fusion.12
  104.1 0.0 all-gather.2.cloned.1.call-done
  104.1 0.0 copy-start.7
  104.2 10.1 %multiply_convert_fusion.1 = (bf16[2048,2048]{1,0:T(8,128)(2,1)S(1)}, f32[2048,2048]{1,0:T(8,128)}) fusion(bf16[1,2,256,2048]{3,2,1,0:T(8,128)(2,1)} %all-gather.2.cloned.1.call-done, f32[2048,256]{1,0:T(8,128)} %fusion.12, bf16[2048,512]{1,0:T(8,128)(2,1)S(1)} %bitcast.46), kind=kOutput, calls=%fused_computation.4 | convolution fusion | flops 2172125184 | bytes 29360128 | tf_op jit(solution)/shard_map/dot_general | solution.py:66
  114.3 0.0 copy-done.7
  114.3 2.6 multiply_reduce_fusion
  116.9 2.3 convolution_bitcast_fusion
  119.3 0.0 copy-start.2
  119.3 13.3 %multiply_convert_fusion = bf16[2048,2048]{1,0:T(8,128)(2,1)} fusion(f32[2048,2048]{1,0:T(8,128)} %get-tuple-element.9, bf16[1,2,256,2048]{3,2,1,0:T(8,128)(2,1)S(1)} %copy-done.7, f32[2048,256]{1,0:T(8,128)S(1)} %get-tuple-element.11), kind=kOutput, calls=%fused_computation.3 | convolution fusion | flops 2186280960 | bytes 28311552 | tf_op jit(solution)/shard_map/dot_general | solution.py:81
  132.6 0.0 copy-done.2
  132.6 5.8 %convolution_bitcast_fusion.1 = f32[1,256,2048]{2,1,0:T(8,128)S(1)} fusion(bf16[2048,2048]{1,0:T(8,128)(2,1)} %multiply_convert_fusion, f32[2048,256]{1,0:T(8,128)S(1)} %copy-done.2, bf16[2048,512]{1,0:T(8,128)(2,1)S(1)} %bitcast.48), kind=kOutput, calls=%fused_computation.8 | convolution fusion | flops 2151153664 | bytes 13631488 | tf_op jit(solution)/shard_map/dot_general | solution.py:83
  138.4 2.2 maximum_bitcast_fusion
  140.6 0.0 reduce-scatter.2.cloned.1.call-update
  140.7 0.7 mul.111
  141.3 5.6 %all-to-all-start.1 = ((f32[64,1,32]{2,1,0:T(1,128)}), f32[64,1,32]{2,1,0:T(1,128)S(1)}, u32[]{:S(2)}, u32[]{:S(2)}) async-start(f32[64,1,32]{2,1,0:T(1,128)} %bitcast.10), calls=%async_computation.1 | async-start | bytes 65536 | tf_op jit(solution)/shard_map/all_to_all | solution.py:74
  146.9 0.0 all-reduce.2.cloned.1.call-start
  147.0 9.0 %fusion.9 = f32[256,256]{1,0:T(8,128)} fusion(bf16[2048,2048]{1,0:T(8,128)(2,1)} %multiply_convert_fusion, f32[2048,256]{1,0:T(8,128)} %fusion.12, bf16[1,2,256,2048]{3,2,1,0:T(8,128)(2,1)} %all-gather.2.cloned.1.call-done, bf16[2048,512]{1,0:T(8,128)(2,1)S(1)} %bitcast.49), kind=kOutput, calls=%fused_computation.29 | convolution fusion | flops 2421686272 | bytes 12845056 | tf_op jit(solution)/shard_map/dot_general | solution.py:90
  155.9 0.0 all-reduce.2.cloned.1.call-update
  156.0 0.5 all-to-all-done.1
  156.4 0.5 broadcast.88
  157.0 0.7 reduce.3
  157.7 0.1 reshape.69
  157.8 0.0 copy-start.1
  157.8 0.0 copy-start.3
  157.8 10.5 %gather_fusion.1 = f32[1024]{0:T(1024)} fusion(f32[2048]{0:T(1024)S(1)} %reshape.69, s32[1024]{0:T(1024)S(1)} %broadcast_clamp_fusion), kind=kCustom, calls=%fused_computation.1 | custom fusion | bytes 12288 | tf_op jit(solution)/shard_map/gather | solution.py:77
  168.3 16.8 %reduce-scatter.2.cloned.1.call-done = f32[1,2,256,512]{3,2,1,0:T(8,128)} async-done(((f32[1,2,256,2048]{3,2,1,0:T(8,128)}), f32[1,2,256,512]{3,2,1,0:T(8,128)}) %reduce-scatter.2.cloned.1.call-update) | async-done | bytes 1048592 | tf_op jit(solution)/shard_map/reduce_scatter | solution.py:95
  185.1 0.0 copy-done.1
  185.1 0.0 copy-done.3
  185.1 3.7 divide_subtract_fusion
  188.8 254.6 %all-reduce.2.cloned.1.call-done = f32[256,256]{1,0:T(8,128)} async-done(((f32[256,256]{1,0:T(8,128)}), f32[256,256]{1,0:T(8,128)}) %all-reduce.2.cloned.1.call-update) | async-done | bytes 262160 | tf_op jit(solution)/shard_map/psum | solution.py:93
  443.3 1.7 copy.25
  (6 shorter events, 0.1 us)
Async XLA Ops:
  7.2 20.9 %copy-start = (bf16[2048,256]{1,0:T(8,128)(2,1)S(1)}, bf16[2048,256]{1,0:T(8,128)(2,1)}, u32[]{:S(2)}) copy-start(bf16[2048,256]{1,0:T(8,128)(2,1)} %param.8) | copy-start | bytes 3145732
  7.2 20.8 %copy-start.6 = (s32[1024,1]{0,1:T(1,128)S(1)}, s32[1024,1]{0,1:T(1,128)}, u32[]{:S(2)}) copy-start(s32[1024,1]{0,1:T(1,128)} %param.10) | copy-start | bytes 12292
  28.1 4.2 copy-start.4
  38.9 63.5 %all-to-all-start = ((bf16[64,32,512]{2,1,0:T(8,128)(2,1)}), bf16[64,32,512]{2,1,0:T(8,128)(2,1)S(1)}, u32[]{:S(2)}, u32[]{:S(2)}) async-start(bf16[64,32,512]{2,1,0:T(8,128)(2,1)} %bitcast.6), calls=%async_computation | async-start | bytes 4194304 | tf_op jit(solution)/shard_map/all_to_all | solution.py:55
  51.0 51.4 %copy-start.5 = (bf16[256,256]{1,0:T(8,128)(2,1)S(1)}, bf16[256,256]{1,0:T(8,128)(2,1)}, u32[]{:S(2)}) copy-start(bf16[256,256]{1,0:T(8,128)(2,1)} %param.12) | copy-start | bytes 393220
  51.1 53.1 %all-gather.2.cloned.1.call-start = ((), (), s32[]{:S(2)}) async-start(), calls=%async_computation.3 | async-start | bytes 2621440 | tf_op jit(solution)/shard_map/all_gather | solution.py:50
  53.2 131.8 %reduce-scatter.2.cloned.1.call-start = ((), (), s32[]{:S(2)}) async-start(), calls=%async_computation.5 | async-start | bytes 5242880 | tf_op jit(solution)/shard_map/reduce_scatter | solution.py:95
  104.1 10.1 %copy-start.7 = (bf16[1,2,256,2048]{3,2,1,0:T(8,128)(2,1)S(1)}, bf16[1,2,256,2048]{3,2,1,0:T(8,128)(2,1)}, u32[]{:S(2)}) copy-start(bf16[1,2,256,2048]{3,2,1,0:T(8,128)(2,1)} %all-gather.2.cloned.1.call-done) | copy-start | bytes 6291460
  119.3 13.3 %copy-start.2 = (f32[2048,256]{1,0:T(8,128)S(1)}, f32[2048,256]{1,0:T(8,128)}, u32[]{:S(2)}) copy-start(f32[2048,256]{1,0:T(8,128)} %fusion.12) | copy-start | bytes 6291460
  141.3 15.1 %all-to-all-start.1 = ((f32[64,1,32]{2,1,0:T(1,128)}), f32[64,1,32]{2,1,0:T(1,128)S(1)}, u32[]{:S(2)}, u32[]{:S(2)}) async-start(f32[64,1,32]{2,1,0:T(1,128)} %bitcast.10), calls=%async_computation.1 | async-start | bytes 65536 | tf_op jit(solution)/shard_map/all_to_all | solution.py:74
  146.9 296.4 %all-reduce.2.cloned.1.call-start = ((), (), s32[]{:S(2)}) async-start(), calls=%async_computation.4 | async-start | bytes 524288 | tf_op jit(solution)/shard_map/psum | solution.py:93
  157.8 27.3 %copy-start.1 = (f32[1,2,256,512]{3,2,1,0:T(8,128)S(1)}, f32[1,2,256,512]{3,2,1,0:T(8,128)}, u32[]{:S(2)}) copy-start(f32[1,2,256,512]{3,2,1,0:T(8,128)} %param.13) | copy-start | bytes 3145732
  157.8 27.3 %copy-start.3 = (f32[1,2,256,512]{3,2,1,0:T(8,128)S(1)}, f32[1,2,256,512]{3,2,1,0:T(8,128)}, u32[]{:S(2)}) copy-start(f32[1,2,256,512]{3,2,1,0:T(8,128)} %param.14) | copy-start | bytes 3145732
Sparse Core Ops, SparseCore 0:
  54.3 33.5 all-gather.1
  140.7 44.3 reduce-scatter.1
  192.0 251.2 all-reduce.1
where the time goes:
time: 452 us
  waiting for transfers between devices  321 us (71%)
  matrix products  44.9 us (10%)
  other arithmetic  36.1 us (8%)
  starting transfers between devices  18 us (4%)
  local copies, waits for them, and re-layouts  17.8 us (4%)
  between operations  13.9 us (3%)
    psum x1, waiting for transfers between devices, on_device(): trunk_grad = lax.psum(trunk_local, ('dp', 'expert'))  255 us
    all_to_all x1, waiting for transfers between devices, on_device(): lax.all_to_all(packed.reshape(experts, capacity, 2 * width), 'expert', sp...  48.9 us
    another operation x3, other arithmetic  18.2 us
    reduce_scatter x1, waiting for transfers between devices, on_device(): grad_shard = lax.psum_scatter(grads, 'dp', scatter_dimension=3, tiled=True)  16.8 us
    dot_general x1, matrix products, on_device(): hidden_grad = jnp.dot(scaled, w_down, preferred_element_type=jnp.float32)  13.3 us
    all_to_all x1, starting transfers between devices, on_device(): lax.all_to_all(packed.reshape(experts, capacity, 2 * width), 'expert', sp...  12.1 us
    gather x1, local copies, waits for them, and re-layouts, on_device(): row_loss = back.reshape(-1)[places]  10.5 us
    dot_general x1, matrix products, on_device(): up_pre = jnp.dot(trunk_out, w_up, preferred_element_type=jnp.float32)  10.1 us
  transfers between devices with their start and end apart: 5, of which 4 were waited for; matrix products, arithmetic and copies ran while one was open for 6% of the time, Pallas kernels for 0%

commit v1 on v0

--- a/solution.py
+++ b/solution.py
@@ -38,6 +38,14 @@
     first_moment,
     second_moment,
 ):
+
+    def case_expand(chunk):
+        shard_axis = "expert"
+        across = "dp"
+        for ix in (across, shard_axis):
+            chunk = lax.psum(chunk, ix)
+        return chunk
+
     rows = sample_index.shape[0]
     width = cell_table.shape[1]
     experts = lax.axis_size("expert")
@@ -90,7 +98,7 @@
     trunk_local = lax.dot_general(
         feats, trunk_slope, (((0,), (0,)), ((), ())), preferred_element_type=jnp.float32
     )
-    trunk_grad = lax.psum(trunk_local, ("dp", "expert"))
+    trunk_grad = case_expand(trunk_local)
     grads = jnp.stack([grad_up, grad_down])[None]
     grad_shard = lax.psum_scatter(grads, "dp", scatter_dimension=3, tiled=True)
     new_params, new_first, new_second = adam_update(

time: 452 us -> 432 us (0.956)
  waiting for transfers between devices: 321 us -> 296 us
    psum x1 -> x2, waiting for transfers between devices: 255 us -> 185 us  [case_expand(): chunk = lax.psum(chunk, ix)]
    reduce_scatter x1, waiting for transfers between devices: 16.8 us -> 52.4 us  [on_device(): grad_shard = lax.psum_scatter(grads, 'dp', scatter_dimension=3, tiled=True)]
    all_to_all x1, waiting for transfers between devices: 0.48 us -> 9.46 us  [on_device(): lax.all_to_all(losses.reshape(experts, capacity), 'expert', split_axis=0,...]
  transfers between devices with their start and end apart: 5 -> 6, of which waited for: 4 -> 5; matrix products, arithmetic and copies ran while one was open for 6% -> 6% of each run, Pallas kernels for 0% -> 0%
where the time goes in v1:
time: 432 us; the launch traced here: 429 us
  waiting for transfers between devices  296 us (69%)
  matrix products  46 us (11%)
  other arithmetic  37.8 us (9%)
  local copies, waits for them, and re-layouts  17.8 us (4%)
  starting transfers between devices  17.8 us (4%)
  between operations  14 us (3%)
    psum x2, waiting for transfers between devices, case_expand(): chunk = lax.psum(chunk, ix)  185 us
    reduce_scatter x1, waiting for transfers between devices, on_device(): grad_shard = lax.psum_scatter(grads, 'dp', scatter_dimension=3, tiled=True)  52.4 us
    all_to_all x1, waiting for transfers between devices, on_device(): lax.all_to_all(packed.reshape(experts, capacity, 2 * width), 'expert', sp...  48.9 us
    another operation x3, other arithmetic  18.2 us
    dot_general x1, matrix products, on_device(): hidden_grad = jnp.dot(scaled, w_down, preferred_element_type=jnp.float32)  13.3 us
    all_to_all x1, starting transfers between devices, on_device(): lax.all_to_all(packed.reshape(experts, capacity, 2 * width), 'expert', sp...  12.1 us
    gather x1, local copies, waits for them, and re-layouts, on_device(): row_loss = back.reshape(-1)[places]  10.5 us
    dot_general x1, matrix products, on_device(): up_pre = jnp.dot(trunk_out, w_up, preferred_element_type=jnp.float32)  10.2 us
  transfers between devices with their start and end apart: 6, of which 5 were waited for; matrix products, arithmetic and copies ran while one was open for 6% of the time, Pallas kernels for 0%

profile of v1, /device:TPU:2, one launch (start us, length us, event | category | flops | bytes accessed | tf_op | source)
XLA Modules:
  0.0 429.3 jit_solution(12817080552622944949)
XLA Ops:
  7.2 0.0 copy-start
  7.2 0.0 copy-start.8
  7.2 0.8 fusion.17
  8.0 0.7 compare_and_fusion
  8.7 0.7 fusion.16
  9.4 18.0 %reduce-window.6 = s32[64,8,128]{2,1,0:T(8,128)S(1)} reduce-window(s32[64,8,128]{2,1,0:T(8,128)S(1)} %fusion.16, s32[]{:T(128)} %constant.20.clone.1), window={size=1x1x128 pad=0_0x0_0x127_0}, to_apply=%region_0.1 | reduce-window | flops 8323072 | bytes 524292 | tf_op jit(solution)/shard_map/reduce-window
  27.4 0.1 slice.28
  27.5 0.1 copy.17
  27.7 0.1 copy.18
  27.8 0.1 broadcast_add_fusion
  27.9 0.0 copy-done.8
  27.9 0.1 fusion.15
  28.0 0.0 copy-done
  28.1 0.0 copy-start.6
  28.1 3.9 gather_fusion
  32.0 0.2 broadcast_select_fusion
  32.2 0.0 copy-done.6
  32.2 6.7 %scatter_custom_fusion = bf16[2048,512]{1,0:T(8,128)(2,1)} fusion(s32[1024]{0:T(1024)S(1)} %bitcast.54, bf16[1024,256]{1,0:T(8,128)(2,1)S(1)} %copy-done.6, bf16[]{:T(256)} %constant.67, bf16[1024,256]{1,0:T(8,128)(2,1)S(1)} %broadcast_select_fusion, bf16[]{:T(256)} %constant.18.clone.1), kind=kCustom, calls=%fused_computation.22 | custom fusion | flops 2097152 | bytes 3145732 | tf_op jit(solution)/shard_map/scatter | solution.py:62
  38.9 12.1 %all-to-all-start = ((bf16[64,32,512]{2,1,0:T(8,128)(2,1)}), bf16[64,32,512]{2,1,0:T(8,128)(2,1)S(1)}, u32[]{:S(2)}, u32[]{:S(2)}) async-start(bf16[64,32,512]{2,1,0:T(8,128)(2,1)} %bitcast.6), calls=%async_computation | async-start | bytes 4194304 | tf_op jit(solution)/shard_map/all_to_all | solution.py:63
  51.0 0.0 copy-start.7
  51.1 0.0 all-gather.2.cloned.1.call-start
  51.1 2.1 convert_element_type.38
  53.2 0.0 all-gather.2.cloned.1.call-update
  53.2 0.2 all-reduce.3.cloned.1.call-start
  53.5 48.9 %all-to-all-done = bf16[64,32,512]{2,1,0:T(8,128)(2,1)S(1)} async-done(((bf16[64,32,512]{2,1,0:T(8,128)(2,1)}), bf16[64,32,512]{2,1,0:T(8,128)(2,1)S(1)}, u32[]{:S(2)}, u32[]{:S(2)}) %all-to-all-start) | async-done | bytes 2097184 | tf_op jit(solution)/shard_map/all_to_all | solution.py:63
  102.4 0.0 copy-start.1
  102.4 0.0 copy-done.7
  102.4 2.0 fusion.12
  104.4 0.0 all-gather.2.cloned.1.call-done
  104.4 0.0 copy-start.9
  104.4 10.2 %multiply_convert_fusion.1 = (bf16[2048,2048]{1,0:T(8,128)(2,1)S(1)}, f32[2048,2048]{1,0:T(8,128)}) fusion(bf16[1,2,256,2048]{3,2,1,0:T(8,128)(2,1)} %all-gather.2.cloned.1.call-done, f32[2048,256]{1,0:T(8,128)} %fusion.12, bf16[2048,512]{1,0:T(8,128)(2,1)S(1)} %bitcast.46), kind=kOutput, calls=%fused_computation.4 | convolution fusion | flops 2172125184 | bytes 29360128 | tf_op jit(solution)/shard_map/dot_general | solution.py:74
  114.6 0.0 copy-done.1
  114.6 0.0 copy-done.9
  114.6 2.6 multiply_reduce_fusion
  117.2 2.3 convolution_bitcast_fusion
  119.5 0.0 copy-start.2
  119.5 0.0 copy-start.4
  119.6 13.3 %multiply_convert_fusion = bf16[2048,2048]{1,0:T(8,128)(2,1)} fusion(f32[2048,2048]{1,0:T(8,128)} %get-tuple-element.9, bf16[1,2,256,2048]{3,2,1,0:T(8,128)(2,1)S(1)} %copy-done.9, f32[2048,256]{1,0:T(8,128)S(1)} %get-tuple-element.11), kind=kOutput, calls=%fused_computation.3 | convolution fusion | flops 2186280960 | bytes 28311552 | tf_op jit(solution)/shard_map/dot_general | solution.py:89
  132.9 0.0 copy-done.2
  132.9 0.0 copy-done.4
  132.9 7.1 %convolution_bitcast_fusion.1 = f32[1,256,2048]{2,1,0:T(8,128)} fusion(bf16[2048,2048]{1,0:T(8,128)(2,1)} %multiply_convert_fusion, f32[2048,256]{1,0:T(8,128)S(1)} %copy-done.4, bf16[2048,512]{1,0:T(8,128)(2,1)S(1)} %bitcast.49), kind=kOutput, calls=%fused_computation.8 | convolution fusion | flops 2151153664 | bytes 13631488 | tf_op jit(solution)/shard_map/dot_general | solution.py:91
  140.0 8.5 %fusion.9 = f32[256,256]{1,0:T(8,128)} fusion(bf16[2048,2048]{1,0:T(8,128)(2,1)} %multiply_convert_fusion, f32[2048,256]{1,0:T(8,128)} %fusion.12, bf16[1,2,256,2048]{3,2,1,0:T(8,128)(2,1)} %all-gather.2.cloned.1.call-done, bf16[2048,512]{1,0:T(8,128)(2,1)} %bitcast.48), kind=kOutput, calls=%fused_computation.29 | convolution fusion | flops 2421686272 | bytes 12845056 | tf_op jit(solution)/shard_map/dot_general | solution.py:98
  148.5 0.0 all-reduce.3.cloned.1.call-update
  148.5 0.0 reduce-scatter.2.cloned.1.call-start
  148.6 3.9 maximum_bitcast_fusion
  152.5 0.0 reduce-scatter.2.cloned.1.call-update
  152.5 0.7 mul.111
  153.2 5.3 %all-to-all-start.1 = ((f32[64,1,32]{2,1,0:T(1,128)}), f32[64,1,32]{2,1,0:T(1,128)S(1)}, u32[]{:S(2)}, u32[]{:S(2)}) async-start(f32[64,1,32]{2,1,0:T(1,128)} %bitcast.10), calls=%async_computation.1 | async-start | bytes 65536 | tf_op jit(solution)/shard_map/all_to_all | solution.py:82
  158.5 0.0 all-reduce.5.cloned.1.call-start
  158.6 9.5 %all-to-all-done.1 = f32[64,1,32]{2,1,0:T(1,128)S(1)} async-done(((f32[64,1,32]{2,1,0:T(1,128)}), f32[64,1,32]{2,1,0:T(1,128)S(1)}, u32[]{:S(2)}, u32[]{:S(2)}) %all-to-all-start.1) | async-done | bytes 8224 | tf_op jit(solution)/shard_map/all_to_all | solution.py:82
  168.1 0.5 broadcast.88
  168.6 0.7 reduce.3
  169.3 0.1 reshape.69
  169.4 0.0 copy-start.3
  169.4 0.0 copy-start.5
  169.4 10.5 %gather_fusion.1 = f32[1024]{0:T(1024)} fusion(f32[2048]{0:T(1024)S(1)} %reshape.69, s32[1024]{0:T(1024)S(1)} %broadcast_clamp_fusion), kind=kCustom, calls=%fused_computation.1 | custom fusion | bytes 12288 | tf_op jit(solution)/shard_map/gather | solution.py:85
  179.9 10.6 %all-reduce.3.cloned.1.call-done = f32[256,256]{1,0:T(8,128)} async-done(((f32[256,256]{1,0:T(8,128)}), f32[256,256]{1,0:T(8,128)}) %all-reduce.3.cloned.1.call-update) | async-done | bytes 262160 | tf_op jit(solution)/shard_map/psum | solution.py:46
  190.5 0.0 all-reduce.5.cloned.1.call-update
  190.5 52.4 %reduce-scatter.2.cloned.1.call-done = f32[1,2,256,512]{3,2,1,0:T(8,128)} async-done(((f32[1,2,256,2048]{3,2,1,0:T(8,128)}), f32[1,2,256,512]{3,2,1,0:T(8,128)}) %reduce-scatter.2.cloned.1.call-update) | async-done | bytes 1048592 | tf_op jit(solution)/shard_map/reduce_scatter | solution.py:103
  242.9 0.0 copy-done.3
  242.9 0.0 copy-done.5
  242.9 3.7 divide_subtract_fusion
  246.6 174.5 %all-reduce.5.cloned.1.call-done = f32[256,256]{1,0:T(8,128)} async-done(((f32[256,256]{1,0:T(8,128)}), f32[256,256]{1,0:T(8,128)}) %all-reduce.5.cloned.1.call-update) | async-done | bytes 262160 | tf_op jit(solution)/shard_map/psum | solution.py:46
  421.1 1.7 copy.26
  (6 shorter events, 0.1 us)
Async XLA Ops:
  7.2 20.9 %copy-start = (bf16[2048,256]{1,0:T(8,128)(2,1)S(1)}, bf16[2048,256]{1,0:T(8,128)(2,1)}, u32[]{:S(2)}) copy-start(bf16[2048,256]{1,0:T(8,128)(2,1)} %param.8) | copy-start | bytes 3145732
  7.2 20.8 %copy-start.8 = (s32[1024,1]{0,1:T(1,128)S(1)}, s32[1024,1]{0,1:T(1,128)}, u32[]{:S(2)}) copy-start(s32[1024,1]{0,1:T(1,128)} %param.10) | copy-start | bytes 12292
  28.1 4.2 copy-start.6
  38.9 63.5 %all-to-all-start = ((bf16[64,32,512]{2,1,0:T(8,128)(2,1)}), bf16[64,32,512]{2,1,0:T(8,128)(2,1)S(1)}, u32[]{:S(2)}, u32[]{:S(2)}) async-start(bf16[64,32,512]{2,1,0:T(8,128)(2,1)} %bitcast.6), calls=%async_computation | async-start | bytes 4194304 | tf_op jit(solution)/shard_map/all_to_all | solution.py:63
  51.0 51.4 %copy-start.7 = (bf16[256,256]{1,0:T(8,128)(2,1)S(1)}, bf16[256,256]{1,0:T(8,128)(2,1)}, u32[]{:S(2)}) copy-start(bf16[256,256]{1,0:T(8,128)(2,1)} %param.12) | copy-start | bytes 393220
  51.1 53.3 %all-gather.2.cloned.1.call-start = ((), (), s32[]{:S(2)}) async-start(), calls=%async_computation.3 | async-start | bytes 2621440 | tf_op jit(solution)/shard_map/all_gather | solution.py:58
  53.2 137.2 %all-reduce.3.cloned.1.call-start = ((), (), s32[]{:S(2)}) async-start(), calls=%async_computation.4 | async-start | bytes 524288 | tf_op jit(solution)/shard_map/psum | solution.py:46
  102.4 12.2 %copy-start.1 = (bf16[64,32,512]{2,1,0:T(8,128)(2,1)}, bf16[64,32,512]{2,1,0:T(8,128)(2,1)S(1)}, u32[]{:S(2)}) copy-start(bf16[64,32,512]{2,1,0:T(8,128)(2,1)S(1)} %all-to-all-done) | copy-start | bytes 6291460
  104.4 10.2 %copy-start.9 = (bf16[1,2,256,2048]{3,2,1,0:T(8,128)(2,1)S(1)}, bf16[1,2,256,2048]{3,2,1,0:T(8,128)(2,1)}, u32[]{:S(2)}) copy-start(bf16[1,2,256,2048]{3,2,1,0:T(8,128)(2,1)} %all-gather.2.cloned.1.call-done) | copy-start | bytes 6291460
  119.5 13.4 %copy-start.2 = (bf16[64,32,512]{2,1,0:T(8,128)(2,1)S(1)}, bf16[64,32,512]{2,1,0:T(8,128)(2,1)}, u32[]{:S(2)}) copy-start(bf16[64,32,512]{2,1,0:T(8,128)(2,1)} %copy-done.1) | copy-start | bytes 6291460
  119.5 13.3 %copy-start.4 = (f32[2048,256]{1,0:T(8,128)S(1)}, f32[2048,256]{1,0:T(8,128)}, u32[]{:S(2)}) copy-start(f32[2048,256]{1,0:T(8,128)} %fusion.12) | copy-start | bytes 6291460
  148.5 94.4 %reduce-scatter.2.cloned.1.call-start = ((), (), s32[]{:S(2)}) async-start(), calls=%async_computation.6 | async-start | bytes 5242880 | tf_op jit(solution)/shard_map/reduce_scatter | solution.py:103
  153.2 14.9 %all-to-all-start.1 = ((f32[64,1,32]{2,1,0:T(1,128)}), f32[64,1,32]{2,1,0:T(1,128)S(1)}, u32[]{:S(2)}, u32[]{:S(2)}) async-start(f32[64,1,32]{2,1,0:T(1,128)} %bitcast.10), calls=%async_computation.1 | async-start | bytes 65536 | tf_op jit(solution)/shard_map/all_to_all | solution.py:82
  158.5 262.6 %all-reduce.5.cloned.1.call-start = ((), (), s32[]{:S(2)}) async-start(), calls=%async_computation.5 | async-start | bytes 524288 | tf_op jit(solution)/shard_map/psum | solution.py:46
  169.4 73.6 %copy-start.3 = (f32[1,2,256,512]{3,2,1,0:T(8,128)S(1)}, f32[1,2,256,512]{3,2,1,0:T(8,128)}, u32[]{:S(2)}) copy-start(f32[1,2,256,512]{3,2,1,0:T(8,128)} %param.13) | copy-start | bytes 3145732
  169.4 73.6 %copy-start.5 = (f32[1,2,256,512]{3,2,1,0:T(8,128)S(1)}, f32[1,2,256,512]{3,2,1,0:T(8,128)}, u32[]{:S(2)}) copy-start(f32[1,2,256,512]{3,2,1,0:T(8,128)} %param.14) | copy-start | bytes 3145732
Sparse Core Ops, SparseCore 0:
  54.3 33.5 all-gather.1
  148.6 41.8 all-reduce.2
  193.2 49.6 reduce-scatter.1
  246.3 174.7 all-reduce.4
